TPU v7x, 32 devices: a whole 2x2x4 slice. The times are simulated.
32 devices in a mesh: rows: 16 (over z, y, x), cols: 2 (over core).
Axes of the slice: x: 2, y: 2, z: 4, core: 2. Of those that a mesh axis runs over, the one named last changes fastest.
Arguments:
- tokens_in: bfloat16 [6304, 768], P(('rows', 'cols')), may hold values from -6 to 6
- ln1_gain: float32 [768], replicated, may hold values from 0.5 to 1.5
- ln1_shift: float32 [768], replicated, may hold values from -4 to 4
- qkv_weight: bfloat16 [768, 2304], P(None, 'cols'), may hold values from -0.21875 to 0.21875
- out_weight: bfloat16 [768, 768], P('cols'), may hold values from -1.75 to 1.75
- ln2_gain: float32 [768], replicated, may hold values from 0.5 to 1.5
- ln2_shift: float32 [768], replicated, may hold values from -4 to 4
- router_weight: bfloat16 [768, 32], replicated, may hold values from -0.4375 to 0.4375
- expert_in: bfloat16 [768, 98304], P(None, ('rows', 'cols')), may hold values from -0.21875 to 0.21875
- expert_out: bfloat16 [98304, 768], P(('rows', 'cols')), may hold values from -0.4375 to 0.4375
- routes: int32 [6304, 2], P(('rows', 'cols')), may hold values from 0 to 31, all different within a row; in each aligned block of 197 rows (0 to 196, 197 to 393, ...) at most 16 rows name the same one
- cotangent: bfloat16 [6304, 768], P(('rows', 'cols')), may hold values from -6 to 6
Outputs:
- output: bfloat16 [6304, 768], P(('rows', 'cols'))
- tokens_grad: bfloat16 [6304, 768], P(('rows', 'cols'))
- ln1_gain_grad: float32 [768], replicated
- ln1_shift_grad: float32 [768], replicated
- qkv_grad: float32 [768, 2304], P(None, 'cols')
- out_grad: float32 [768, 768], P('cols')
- ln2_gain_grad: float32 [768], replicated
- ln2_shift_grad: float32 [768], replicated
- router_grad: float32 [768, 32], replicated
- expert_in_grad: float32 [768, 98304], P(None, ('rows', 'cols'))
- expert_out_grad: float32 [98304, 768], P(('rows', 'cols'))
Inputs may be any that keep to these rules, and one draw needn't show every extreme that they name: `routes`: the two experts of a token differ. Among the tokens of one device (aligned blocks of 197 rows) each expert is named by at most 16 assignments, a bound that some block reaches.
All inputs are finite; a program needn't handle non-finite values.
Results may differ from a plain program's by a relative error of at most 0.022.
Values may be sent and summed in bfloat16 or wider, within the bound.
A program may use at most 192 MiB of HBM per device.

v0:
```python
import jax
import jax.numpy as jnp
from jax import lax
from jax.sharding import PartitionSpec as P

DH = 64
FF = 3072
SEQ = 197
EPSILON = 1e-06


def layer_norm(values, norm_gain, norm_shift):
    average = jnp.mean(values, axis=-1, keepdims=True)
    centred = values - average
    variance = jnp.mean(centred * centred, axis=-1, keepdims=True)
    return centred * lax.rsqrt(variance + EPSILON) * norm_gain + norm_shift


def gelu_slope(pre_act):
    normal_cdf = 0.5 * (1.0 + jax.scipy.special.erf(pre_act * 0.7071067811865476))
    density = jnp.exp(-0.5 * pre_act * pre_act) * 0.3989422804014327
    return normal_cdf + pre_act * density


def dot_rows(first_side, second_side):
    return lax.dot_general(
        first_side, second_side, (((0,), (0,)), ((), ())), preferred_element_type=jnp.float32
    )


def dot_last(first_side, second_side):
    return lax.dot_general(
        first_side, second_side, (((1,), (1,)), ((), ())), preferred_element_type=jnp.float32
    )


def attention_scores(queries, keys_all, score_scale):
    scores = jnp.einsum("nqhd,nkhd->nhqk", queries, keys_all, preferred_element_type=jnp.float32)
    return scores * score_scale


def body(
    tokens_in,
    ln1_gain,
    ln1_shift,
    qkv_weight,
    out_weight,
    ln2_gain,
    ln2_shift,
    router_weight,
    expert_in,
    expert_out,
    routes,
    cotangent,
):
    local_rows = tokens_in.shape[0]
    model_width = tokens_in.shape[1]
    experts = router_weight.shape[1]
    capacity = max(2, 8 * local_rows // (3 * experts))
    heads_local = qkv_weight.shape[1] // (3 * DH)
    score_scale = DH ** (-0.5)
    row_count = lax.axis_size("rows")
    row_place = lax.axis_index("rows")
    col_place = lax.axis_index("cols")
    per_device = max(1, experts // row_count)
    copies = max(1, row_count // experts)
    slots = per_device * capacity
    piece_half = expert_in.shape[1]
    piece_whole = piece_half * lax.axis_size("cols")
    arrived_rows = row_count * slots
    tokens_f = tokens_in.astype(jnp.float32)
    normed_low = layer_norm(tokens_f, ln1_gain, ln1_shift).astype(jnp.bfloat16)
    gathered = lax.all_gather(normed_low, "cols", axis=0, tiled=True)
    pair_rows = gathered.shape[0]
    images = pair_rows // SEQ
    qkv_low = jnp.dot(gathered, qkv_weight, preferred_element_type=jnp.float32).astype(jnp.bfloat16)
    head_split = qkv_low.reshape(images, SEQ, heads_local, 3, DH)
    queries = head_split[:, :, :, 0]
    keys_all = head_split[:, :, :, 1]
    values_all = head_split[:, :, :, 2]
    scores = attention_scores(queries, keys_all, score_scale)
    score_peak = jnp.max(scores, axis=-1, keepdims=True)
    log_total = score_peak + jnp.log(jnp.sum(jnp.exp(scores - score_peak), axis=-1, keepdims=True))
    weights_low = jnp.exp(scores - log_total).astype(jnp.bfloat16)
    context = jnp.einsum(
        "nhqk,nkhd->nqhd", weights_low, values_all, preferred_element_type=jnp.float32
    )
    context_low = context.astype(jnp.bfloat16).reshape(pair_rows, heads_local * DH)
    row_block = context_low
    attn_out = lax.psum_scatter(
        jnp.dot(row_block, out_weight, preferred_element_type=jnp.float32),
        "cols",
        scatter_dimension=0,
        tiled=True,
    )
    hidden_one = tokens_f + attn_out
    mixed_low = layer_norm(hidden_one, ln2_gain, ln2_shift).astype(jnp.bfloat16)
    logits = jnp.dot(mixed_low, router_weight, preferred_element_type=jnp.float32)
    router_probs = jax.nn.softmax(logits, axis=-1)
    expert_ids = jnp.arange(experts, dtype=jnp.int32)
    chosen = (routes[:, :, None] == expert_ids[None, None, :]).astype(jnp.float32)
    gate_values = jnp.sum(router_probs[:, None, :] * chosen, axis=-1)
    flat_ids = routes.reshape(-1)
    flat_hot = (flat_ids[:, None] == expert_ids[None, :]).astype(jnp.int32)
    slot_ranks = jnp.sum(jnp.cumsum(flat_hot, axis=0) * flat_hot, axis=1) - 1
    first_device = flat_ids // per_device * copies
    slot_index = flat_ids % per_device * capacity + slot_ranks
    copy_ids = jnp.arange(copies, dtype=jnp.int32)
    targets = ((first_device[:, None] + copy_ids[None, :]) * slots + slot_index[:, None]).reshape(
        -1
    )
    grad_out = cotangent.astype(jnp.float32)
    grad_slots = (
        (gate_values[:, :, None] * grad_out[:, None, :])
        .astype(jnp.bfloat16)
        .reshape(2 * local_rows, model_width)
    )
    rows_send = (
        jnp.zeros((arrived_rows, model_width), jnp.bfloat16)
        .at[targets]
        .set(jnp.repeat(mixed_low, 2 * copies, axis=0))
    )
    grads_send = (
        jnp.zeros((arrived_rows, model_width), jnp.bfloat16)
        .at[targets]
        .set(jnp.repeat(grad_slots, copies, axis=0))
    )
    arrived, grad_result = (
        lax.all_to_all(
            rows_send.reshape(row_count, slots, model_width),
            "rows",
            split_axis=0,
            concat_axis=0,
            tiled=True,
        ),
        lax.all_to_all(
            grads_send.reshape(row_count, slots, model_width),
            "rows",
            split_axis=0,
            concat_axis=0,
            tiled=True,
        ),
    )
    arrived = arrived.reshape(arrived_rows, model_width)
    grad_result = grad_result.reshape(arrived_rows, model_width)
    unit_base = row_place % copies * piece_whole
    both_rows, both_grads = (
        lax.all_gather(arrived, "cols", axis=0, tiled=True),
        lax.all_gather(grad_result, "cols", axis=0, tiled=True),
    )
    slot_local = jnp.arange(both_rows.shape[0], dtype=jnp.int32) % slots // capacity
    unit_local = (
        unit_base + col_place * piece_half + jnp.arange(piece_half, dtype=jnp.int32)
    ) // FF
    mask = (slot_local[:, None] == unit_local[None, :]).astype(jnp.float32)
    pre_act = jnp.dot(both_rows, expert_in, preferred_element_type=jnp.float32) * mask
    act_low = jax.nn.gelu(pre_act, approximate=False).astype(jnp.bfloat16)
    result_low = lax.psum_scatter(
        jnp.dot(act_low, expert_out, preferred_element_type=jnp.float32).astype(jnp.bfloat16),
        "cols",
        scatter_dimension=0,
        tiled=True,
    )
    grad_act = dot_last(both_grads, expert_out)
    grad_pre_low = (grad_act * gelu_slope(pre_act) * mask).astype(jnp.bfloat16)
    first_grad = dot_rows(both_rows, grad_pre_low)
    second_grad = dot_rows(act_low, both_grads)
    grad_arrived = lax.psum_scatter(
        dot_last(grad_pre_low, expert_in).astype(jnp.bfloat16),
        "cols",
        scatter_dimension=0,
        tiled=True,
    )
    returned = lax.all_to_all(
        result_low.reshape(row_count, slots, model_width),
        "rows",
        split_axis=0,
        concat_axis=0,
        tiled=True,
    )
    returned = returned.reshape(arrived_rows, model_width)
    picked = jnp.sum(
        returned[targets].reshape(local_rows, 2, copies, model_width).astype(jnp.float32), axis=2
    )
    output = (hidden_one + jnp.sum(gate_values[:, :, None] * picked, axis=1)).astype(jnp.bfloat16)
    grad_gates = jnp.sum(grad_out[:, None, :] * picked, axis=-1)
    grad_sent = lax.all_to_all(
        grad_arrived.reshape(row_count, slots, model_width),
        "rows",
        split_axis=0,
        concat_axis=0,
        tiled=True,
    )
    grad_sent = grad_sent.reshape(arrived_rows, model_width)
    grad_mixed_experts = jnp.sum(
        grad_sent[targets].reshape(local_rows, 2 * copies, model_width).astype(jnp.float32), axis=1
    )
    gate_term = jnp.sum(grad_gates * gate_values, axis=-1, keepdims=True)
    grad_probs = jnp.sum(chosen * grad_gates[:, :, None], axis=1)
    grad_logits_low = (router_probs * (grad_probs - gate_term)).astype(jnp.bfloat16)
    router_grad = dot_rows(mixed_low, grad_logits_low)
    grad_mixed = dot_last(grad_logits_low, router_weight) + grad_mixed_experts
    unused_two, norm_two_back = jax.vjp(layer_norm, hidden_one, ln2_gain, ln2_shift)
    grad_hidden_part, ln2_gain_grad, ln2_shift_grad = norm_two_back(grad_mixed)
    grad_hidden = grad_out + grad_hidden_part
    grad_attn_low = grad_hidden.astype(jnp.bfloat16)
    grad_attn_all = lax.all_gather(grad_attn_low, "cols", axis=0, tiled=True)
    out_grad = dot_rows(context_low, grad_attn_all)
    grad_context = (
        dot_last(grad_attn_all, out_weight)
        .astype(jnp.bfloat16)
        .reshape(images, SEQ, heads_local, DH)
    )
    scores_again = attention_scores(queries, keys_all, score_scale)
    attn_probs = jnp.exp(scores_again - log_total)
    probs_low = attn_probs.astype(jnp.bfloat16)
    grad_values = jnp.einsum(
        "nhqk,nqhd->nkhd", probs_low, grad_context, preferred_element_type=jnp.float32
    )
    grad_weights = jnp.einsum(
        "nqhd,nkhd->nhqk", grad_context, values_all, preferred_element_type=jnp.float32
    )
    row_term = jnp.sum(grad_weights * attn_probs, axis=-1, keepdims=True)
    grad_scores = (attn_probs * (grad_weights - row_term)).astype(jnp.bfloat16)
    grad_queries = (
        jnp.einsum("nhqk,nkhd->nqhd", grad_scores, keys_all, preferred_element_type=jnp.float32)
        * score_scale
    )
    grad_keys = (
        jnp.einsum("nhqk,nqhd->nkhd", grad_scores, queries, preferred_element_type=jnp.float32)
        * score_scale
    )
    grad_qkv = (
        jnp.stack([grad_queries, grad_keys, grad_values], axis=3)
        .astype(jnp.bfloat16)
        .reshape(pair_rows, 3 * heads_local * DH)
    )
    qkv_grad = dot_rows(gathered, grad_qkv)
    row_block = grad_qkv
    grad_normed = lax.psum_scatter(
        dot_last(row_block, qkv_weight).astype(jnp.bfloat16),
        "cols",
        scatter_dimension=0,
        tiled=True,
    ).astype(jnp.float32)
    unused_one, norm_one_back = jax.vjp(layer_norm, tokens_f, ln1_gain, ln1_shift)
    grad_tokens_part, ln1_gain_grad, ln1_shift_grad = norm_one_back(grad_normed)
    tokens_grad = (grad_hidden + grad_tokens_part).astype(jnp.bfloat16)
    qkv_grad, out_grad = lax.psum((qkv_grad, out_grad), "rows")
    router_grad, ln1_gain_grad, ln1_shift_grad, ln2_gain_grad, ln2_shift_grad = lax.psum(
        (router_grad, ln1_gain_grad, ln1_shift_grad, ln2_gain_grad, ln2_shift_grad),
        ("rows", "cols"),
    )
    return (
        output,
        tokens_grad,
        ln1_gain_grad,
        ln1_shift_grad,
        qkv_grad,
        out_grad,
        ln2_gain_grad,
        ln2_shift_grad,
        router_grad,
        first_grad,
        second_grad,
    )


def solution(mesh):
    in_specs = (
        P(("rows", "cols"), None),
        P(),
        P(),
        P(None, "cols"),
        P("cols", None),
        P(),
        P(),
        P(),
        P(None, ("rows", "cols")),
        P(("rows", "cols"), None),
        P(("rows", "cols"), None),
        P(("rows", "cols"), None),
    )
    out_specs = (
        P(("rows", "cols"), None),
        P(("rows", "cols"), None),
        P(),
        P(),
        P(None, "cols"),
        P("cols", None),
        P(),
        P(),
        P(),
        P(None, ("rows", "cols")),
        P(("rows", "cols"), None),
    )
    return jax.shard_map(body, mesh=mesh, in_specs=in_specs, out_specs=out_specs, check_vma=False)
```

profile of v0, /device:TPU:0, one launch (start us, length us, event | category | flops | bytes accessed | tf_op | source)
XLA Modules:
  0.0 595.0 jit_solution(453533763309978735)
XLA Ops:
  14.9 2.8 reshape.405
  17.7 7.0 %fusion.72 = (bf16[2,197,6,1,64]{4,3,2,1,0:T(2,128)(2,1)S(1)}, bf16[2,197,6,1,64]{4,3,2,1,0:T(2,128)(2,1)}, bf16[2,197,6,1,64]{4,3,2,1,0:T(2,128)(2,1)}) fusion(bf16[2,197,6,3,64]{4,3,2,1,0:T(4,128)(2,1)} %reshape.405), kind=kLoop, calls=%fused_computation.161 | loop fusion | bytes 1815552 | tf_op jit(solution)/shard_map/slice | solution.py:78
  27.2 3.7 copy.122
  39.8 4.9 fusion
  56.2 3.9 scatter_custom_fusion
  60.0 8.3 %all-to-all-start = ((bf16[16,32,768]{2,1,0:T(8,128)(2,1)}), bf16[16,32,768]{2,1,0:T(8,128)(2,1)}, u32[]{:S(2)}, u32[]{:S(2)}) async-start(bf16[16,32,768]{2,1,0:T(8,128)(2,1)} %bitcast.8), calls=%async_computation | async-start | bytes 1572864 | tf_op jit(solution)/shard_map/all_to_all | solution.py:129
  72.2 15.5 %all-to-all-done = bf16[16,32,768]{2,1,0:T(8,128)(2,1)} async-done(((bf16[16,32,768]{2,1,0:T(8,128)(2,1)}), bf16[16,32,768]{2,1,0:T(8,128)(2,1)}, u32[]{:S(2)}, u32[]{:S(2)}) %all-to-all-start) | async-done | bytes 786464 | tf_op jit(solution)/shard_map/all_to_all | solution.py:129
  88.0 3.2 scatter_custom_fusion.1
  91.2 4.9 all-to-all-start.2
  96.2 18.6 %all-to-all-done.2 = bf16[16,32,768]{2,1,0:T(8,128)(2,1)S(1)} async-done(((bf16[16,32,768]{2,1,0:T(8,128)(2,1)}), bf16[16,32,768]{2,1,0:T(8,128)(2,1)S(1)}, u32[]{:S(2)}, u32[]{:S(2)}) %all-to-all-start.2) | async-done | bytes 786464 | tf_op jit(solution)/shard_map/all_to_all | solution.py:136
  115.8 35.3 %fusion.5 = (bf16[1024,3072]{1,0:T(8,128)(2,1)S(1)}, f32[1024,3072]{1,0:T(8,128)}) fusion(s32[3072]{0:T(1024)S(1)} %add_select_fusion, s32[1024]{0:T(1024)S(1)} %add_select_fusion.1, bf16[1024,768]{1,0:T(8,128)(2,1)} %all-gather.5.cloned.1.call-done, bf16[768,3072]{1,0:T(8,128)(2,1)} %param.20), kind=kOutput, calls=%fused_computation.11 | convolution fusion | flops 5042601984 | bytes 25182208 | tf_op jit(solution)/shard_map/dot_general | solution.py:156
  153.8 8.5 %convolution_convert_fusion.2 = bf16[1024,768]{1,0:T(8,128)(2,1)} fusion(bf16[1024,3072]{1,0:T(8,128)(2,1)S(1)} %get-tuple-element.37, bf16[3072,768]{1,0:T(8,128)(2,1)} %param.21), kind=kOutput, calls=%fused_computation.39 | convolution fusion | flops 4832624640 | bytes 12582912 | tf_op jit(solution)/shard_map/dot_general | solution.py:159
  162.3 8.7 %reduce-scatter.9.cloned.1.call-start = ((), (), s32[]{:S(2)}) async-start(), calls=%async_computation.9 | async-start | bytes 2359296 | tf_op jit(solution)/shard_map/reduce_scatter | solution.py:168
  171.1 12.0 %fusion.2 = bf16[1024,3072]{1,0:T(8,128)(2,1)S(1)} fusion(f32[1024,3072]{1,0:T(8,128)} %get-tuple-element.38, bf16[1024,768]{1,0:T(8,128)(2,1)} %all-gather.7.cloned.1.call-done, bf16[3072,768]{1,0:T(8,128)(2,1)} %param.21, s32[3072]{0:T(1024)S(1)} %add_select_fusion, s32[1024]{0:T(1024)S(1)} %add_select_fusion.1), kind=kOutput, calls=%fused_computation.8 | convolution fusion | flops 4872732672 | bytes 25182208 | tf_op jit(solution)/shard_map/dot_general | solution.py:32
  185.8 6.3 %convolution_convert_fusion.1 = bf16[1024,768]{1,0:T(8,128)(2,1)} fusion(bf16[1024,3072]{1,0:T(8,128)(2,1)S(1)} %fusion.2, bf16[768,3072]{1,0:T(8,128)(2,1)S(1)} %bitcast.115), kind=kOutput, calls=%fused_computation.38 | convolution fusion | flops 4832624640 | bytes 12582912 | tf_op jit(solution)/shard_map/dot_general | solution.py:32
  192.1 5.2 all-to-all-start.1
  197.2 3.5 reduce-scatter.9.cloned.1.call-done
  200.8 15.2 %all-to-all-done.1 = bf16[16,32,768]{2,1,0:T(8,128)(2,1)S(1)} async-done(((bf16[16,32,768]{2,1,0:T(8,128)(2,1)}), bf16[16,32,768]{2,1,0:T(8,128)(2,1)S(1)}, u32[]{:S(2)}, u32[]{:S(2)}) %all-to-all-start.1) | async-done | bytes 786464 | tf_op jit(solution)/shard_map/all_to_all | solution.py:174
  216.0 4.9 all-to-all-start.3
  225.4 2.8 reshape.365
  228.2 4.7 multiply_reduce_fusion.2
  234.1 5.3 all-to-all-done.3
  242.1 2.8 reshape.366
  260.9 3.2 fusion.22
  270.2 4.6 fusion.75
  276.4 10.0 %fusion.79 = f32[3072,768]{1,0:T(8,128)} fusion(bf16[1024,3072]{1,0:T(8,128)(2,1)} %copy-done.44, bf16[1024,768]{1,0:T(8,128)(2,1)} %all-gather.7.cloned.1.call-done), kind=kOutput, calls=%fused_computation.168 | convolution fusion | flops 4831838208 | bytes 17301504 | tf_op jit(solution)/shard_map/dot_general | solution.py:26
  287.7 3.4 fusion.1
  294.5 9.9 %fusion.78 = f32[768,3072]{1,0:T(8,128)} fusion(bf16[1024,768]{1,0:T(8,128)(2,1)} %all-gather.5.cloned.1.call-done, bf16[1024,3072]{1,0:T(8,128)(2,1)} %copy-done.43), kind=kOutput, calls=%fused_computation.167 | convolution fusion | flops 4831838208 | bytes 17301504 | tf_op jit(solution)/shard_map/dot_general | solution.py:26
  307.3 40.2 %all-reduce.5 = (f32[768]{0:T(1024)}, f32[768]{0:T(1024)}, f32[768]{0:T(1024)}, f32[768]{0:T(1024)}) all-reduce(f32[768]{0:T(1024)S(1)} %get-tuple-element.15, f32[768]{0:T(1024)S(1)} %get-tuple-element.18, f32[768]{0:T(1024)S(1)} %get-tuple-element.11, ...), channel_id=1, replica_groups=mesh['rows'=16,'cols'=2] {'rows','cols'}, use_global_device_ids=true, to_apply=%region_29.30 | all-reduce | flops 3072 | bytes 24576 | tf_op jit(solution)/shard_map/psum | solution.py:250
  348.6 46.3 %all-reduce.10.cloned.1.call-done = f32[768,32]{0,1:T(8,128)} async-done(((f32[768,32]{0,1:T(8,128)}), f32[768,32]{0,1:T(8,128)}) %all-reduce.10.cloned.1.call-update) | async-done | bytes 98320 | tf_op jit(solution)/shard_map/psum | solution.py:250
  394.8 187.2 %all-reduce.12.cloned.1.call-done = (f32[768,1152]{1,0:T(8,128)}, f32[384,768]{1,0:T(8,128)}) async-done(((f32[768,1152]{1,0:T(8,128)}, f32[384,768]{1,0:T(8,128)}), (f32[768,1152]{1,0:T(8,128)}, f32[384,768]{1,0:T(8,128)})) %all-reduce.12.cloned.1.call-update) | async-done | bytes 4718608 | tf_op jit(solution)/shard_map/psum | solution.py:249
  582.0 4.1 copy.130
  (201 shorter events, 82.3 us)
Async XLA Ops:
  35.1 12.4 %copy-start.31 = (s32[197,2]{0,1:T(2,128)S(1)}, s32[197,2]{0,1:T(2,128)}, u32[]{:S(2)}) copy-start(s32[197,2]{0,1:T(2,128)} %param.22) | copy-start | bytes 4732
  36.0 13.5 %copy-start.42 = (u32[32]{0:T(128)S(1)}, u32[32]{0:T(128)}, u32[]{:S(2)}) copy-start(u32[32]{0:T(128)} %constant.193) | copy-start | bytes 388
  36.0 16.9 %copy-start.5 = (bf16[197,768]{1,0:T(8,128)(2,1)S(1)}, bf16[197,768]{1,0:T(8,128)(2,1)}, u32[]{:S(2)}) copy-start(bf16[197,768]{1,0:T(8,128)(2,1)} %param.12) | copy-start | bytes 907780
  37.1 16.9 %copy-start.28 = (f32[768]{0:T(1024)S(1)}, f32[768]{0:T(1024)}, u32[]{:S(2)}) copy-start(f32[768]{0:T(1024)} %param.17) | copy-start | bytes 9220
  37.1 16.9 %copy-start.41 = (f32[768]{0:T(1024)S(1)}, f32[768]{0:T(1024)}, u32[]{:S(2)}) copy-start(f32[768]{0:T(1024)} %param.18) | copy-start | bytes 9220
  45.4 5.4 collective-permute-start
  47.9 20.5 %copy-start.9 = (bf16[197,768]{1,0:T(8,128)(2,1)S(1)}, bf16[197,768]{1,0:T(8,128)(2,1)}, u32[]{:S(2)}) copy-start(bf16[197,768]{1,0:T(8,128)(2,1)} %param.23) | copy-start | bytes 907780
  53.4 18.8 %copy-start.39 = (f32[197]{0:T(256)}, f32[197]{0:T(256)S(1)}, u32[]{:S(2)}) copy-start(f32[197]{0:T(256)S(1)} %multiply_reduce_fusion.6) | copy-start | bytes 2368
  53.4 18.5 %copy-start.25 = (bf16[768,32]{0,1:T(8,128)(2,1)S(1)}, bf16[768,32]{0,1:T(8,128)(2,1)}, u32[]{:S(2)}) copy-start(bf16[768,32]{0,1:T(8,128)(2,1)} %param.19) | copy-start | bytes 147460
  53.9 18.2 %copy-start.34 = (f32[197]{0:T(256)}, f32[197]{0:T(256)S(1)}, u32[]{:S(2)}) copy-start(f32[197]{0:T(256)S(1)} %fusion.67) | copy-start | bytes 2368
  54.1 33.6 %copy-start.11 = (bf16[197,768]{1,0:T(8,128)(2,1)}, bf16[197,768]{1,0:T(8,128)(2,1)S(1)}, u32[]{:S(2)}) copy-start(bf16[197,768]{1,0:T(8,128)(2,1)S(1)} %add_convert_fusion.2) | copy-start | bytes 907780
  60.0 27.7 %all-to-all-start = ((bf16[16,32,768]{2,1,0:T(8,128)(2,1)}), bf16[16,32,768]{2,1,0:T(8,128)(2,1)}, u32[]{:S(2)}, u32[]{:S(2)}) async-start(bf16[16,32,768]{2,1,0:T(8,128)(2,1)} %bitcast.8), calls=%async_computation | async-start | bytes 1572864 | tf_op jit(solution)/shard_map/all_to_all | solution.py:129
  68.3 47.4 %all-gather.5.cloned.1.call-start = ((), (), s32[]{:S(2)}) async-start(), calls=%async_computation.6 | async-start | bytes 2359296 | tf_op jit(solution)/shard_map/all_gather | solution.py:148
  72.2 15.5 %copy-start.36 = (f32[197]{0:T(256)}, f32[197]{0:T(256)S(1)}, u32[]{:S(2)}) copy-start(f32[197]{0:T(256)S(1)} %fusion.55) | copy-start | bytes 2368
  91.2 23.5 %all-to-all-start.2 = ((bf16[16,32,768]{2,1,0:T(8,128)(2,1)}), bf16[16,32,768]{2,1,0:T(8,128)(2,1)S(1)}, u32[]{:S(2)}, u32[]{:S(2)}) async-start(bf16[16,32,768]{2,1,0:T(8,128)(2,1)} %bitcast.107), calls=%async_computation.3 | async-start | bytes 1572864 | tf_op jit(solution)/shard_map/all_to_all | solution.py:136
  96.1 74.9 %all-gather.7.cloned.1.call-start = ((), (), s32[]{:S(2)}) async-start(), calls=%async_computation.8 | async-start | bytes 2359296 | tf_op jit(solution)/shard_map/all_gather | solution.py:149
  115.7 76.4 %reduce-scatter.7.cloned.1.call-start = ((), (), s32[]{:S(2)}) async-start(), calls=%async_computation.7 | async-start | bytes 2359296 | tf_op jit(solution)/shard_map/reduce_scatter | solution.py:158
  153.8 32.0 %slice-start = ((s8[4718592]{0:T(1024)(128)(4,1)}), s8[524288]{0:T(1024)(128)(4,1)S(1)}, s32[]{:S(2)}) async-start(s8[4718592]{0:T(1024)(128)(4,1)} %bitcast.114), calls=%async_computation.12 | async-start | bytes 1048576
  162.3 38.5 %reduce-scatter.9.cloned.1.call-start = ((), (), s32[]{:S(2)}) async-start(), calls=%async_computation.9 | async-start | bytes 2359296 | tf_op jit(solution)/shard_map/reduce_scatter | solution.py:168
  171.1 14.7 %slice-start.1 = ((s8[4718592]{0:T(1024)(128)(4,1)}), s8[4194304]{0:T(1024)(128)(4,1)S(1)}, s32[]{:S(2)}) async-start(s8[4718592]{0:T(1024)(128)(4,1)} %bitcast.114), calls=%async_computation.13 | async-start | bytes 8388608
  192.1 23.9 %all-to-all-start.1 = ((bf16[16,32,768]{2,1,0:T(8,128)(2,1)}), bf16[16,32,768]{2,1,0:T(8,128)(2,1)S(1)}, u32[]{:S(2)}, u32[]{:S(2)}) async-start(bf16[16,32,768]{2,1,0:T(8,128)(2,1)} %bitcast.109), calls=%async_computation.2 | async-start | bytes 1572864 | tf_op jit(solution)/shard_map/all_to_all | solution.py:174
  216.0 23.5 %all-to-all-start.3 = ((bf16[16,32,768]{2,1,0:T(8,128)(2,1)}), bf16[16,32,768]{2,1,0:T(8,128)(2,1)S(1)}, u32[]{:S(2)}, u32[]{:S(2)}) async-start(bf16[16,32,768]{2,1,0:T(8,128)(2,1)} %bitcast.108), calls=%async_computation.5 | async-start | bytes 1572864 | tf_op jit(solution)/shard_map/all_to_all | solution.py:187
  220.9 174.0 %all-reduce.10.cloned.1.call-start = ((), (), s32[]{:S(2)}) async-start(), calls=%async_computation.10 | async-start | bytes 196608 | tf_op jit(solution)/shard_map/psum | solution.py:250
  232.8 15.6 %copy-start.4 = (f32[197,768]{1,0:T(8,128)S(1)}, f32[197,768]{1,0:T(8,128)}, u32[]{:S(2)}) copy-start(f32[197,768]{1,0:T(8,128)} %copy-done.3) | copy-start | bytes 1815556
  274.9 307.1 %all-reduce.12.cloned.1.call-start = ((), (), s32[]{:S(2)}) async-start(), calls=%async_computation.11 | async-start | bytes 9437184 | tf_op jit(solution)/shard_map/psum | solution.py:249
  291.8 14.7 %copy-start.6 = (bf16[197,768]{1,0:T(8,128)(2,1)S(1)}, bf16[197,768]{1,0:T(8,128)(2,1)}, u32[]{:S(2)}) copy-start(bf16[197,768]{1,0:T(8,128)(2,1)} %param.12) | copy-start | bytes 907780
  291.8 14.7 %copy-start.27 = (f32[768]{0:T(1024)S(1)}, f32[768]{0:T(1024)}, u32[]{:S(2)}) copy-start(f32[768]{0:T(1024)} %param.13) | copy-start | bytes 9220
  291.8 14.7 %copy-start.30 = (f32[197]{0:T(256)S(1)}, f32[197]{0:T(256)}, u32[]{:S(2)}) copy-start(f32[197]{0:T(256)} %copy-done.29) | copy-start | bytes 2368
  291.8 15.0 %copy-start.38 = (f32[197]{0:T(256)S(1)}, f32[197]{0:T(256)}, u32[]{:S(2)}) copy-start(f32[197]{0:T(256)} %copy-done.37) | copy-start | bytes 2368
  291.8 15.0 %copy-start.33 = (f32[197]{0:T(256)S(1)}, f32[197]{0:T(256)}, u32[]{:S(2)}) copy-start(f32[197]{0:T(256)} %copy-done.32) | copy-start | bytes 2368
  291.8 55.6 %copy-start.8 = (f32[197,768]{1,0:T(8,128)S(1)}, f32[197,768]{1,0:T(8,128)}, u32[]{:S(2)}) copy-start(f32[197,768]{1,0:T(8,128)} %copy-done.7) | copy-start | bytes 1815556
  291.8 12.5 %collective-permute-start.1 = (bf16[3,768]{1,0:T(4,128)(2,1)S(1)}, bf16[3,768]{1,0:T(4,128)(2,1)S(1)}, u32[]{:S(2)}, u32[]{:S(2)}) collective-permute-start(bf16[3,768]{1,0:T(4,128)(2,1)S(1)} %slice.34), channel_id=1, source_target_pairs={{0,1},{2,3},{4,5},{6,7},{8,9},{10,11},{12,13},{14,15},{16,17},{18,... | collective-permute-start | bytes 13832
  (27 other events, 107.2 us)
Sparse Core Ops, SparseCore 0:
  87.9 9.0 all-gather.4
  115.8 9.0 all-gather.6
  162.4 8.3 reduce-scatter.6
  192.2 8.5 reduce-scatter.8
  275.0 119.7 all-reduce.9
  401.0 180.9 all-reduce.11
where the time goes:
time: 605 us; the launch traced here: 595 us
  waiting for transfers between devices  292 us (48%)
  matrix products  103 us (17%)
  local copies, waits for them, and re-layouts  68.5 us (11%)
  blocking collectives  53.4 us (9%)
  starting transfers between devices  36.9 us (6%)
  other arithmetic  25.5 us (4%)
  between operations  16.1 us (3%)
    psum x1, waiting for transfers between devices, body(): qkv_grad, out_grad = lax.psum((qkv_grad, out_grad), 'rows')  187 us
    psum x1, waiting for transfers between devices, body(): lax.psum((router_grad, ln1_gain_grad, ln1_shift_grad, ln2_gain_grad, ln2_...  46.3 us
    psum x1, blocking collectives, body(): lax.psum((router_grad, ln1_gain_grad, ln1_shift_grad, ln2_gain_grad, ln2_...  40.2 us
    dot_general x1, matrix products, body(): jnp.dot(both_rows, expert_in, preferred_element_type=jnp.float32) * mask  35.3 us
    unnamed x108, local copies, waits for them, and re-layouts  30.5 us
    dot_general x5, matrix products, dot_rows(): lax.dot_general(first_side, second_side, (((0,), (0,)), ((), ())), prefer...  26.8 us
    dot_general x5, matrix products, dot_last(): lax.dot_general(first_side, second_side, (((1,), (1,)), ((), ())), prefer...  22.5 us
    all_to_all x1, waiting for transfers between devices, body(): lax.all_to_all(grads_send.reshape(row_count, slots, model_width), 'rows',...  18.6 us
  transfers between devices with their start and end apart: 12, of which 7 were waited for; matrix products, arithmetic and copies ran while one was open for 19% of the time, Pallas kernels for 0%

commit v1 on v0

--- a/solution.py
+++ b/solution.py
@@ -7,6 +7,22 @@
 FF = 3072
 SEQ = 197
 EPSILON = 1e-06
+
+
+def exchange_in_pairs(x, axis, split, join):
+    ways, here = (lax.axis_size(axis), lax.axis_index(axis))
+    width = x.shape[split] // ways
+    dims = list(x.shape)
+    dims[split] = width
+    height = dims[join]
+    dims[join] = height * ways
+    full = jnp.zeros(dims, x.dtype)
+    for mask in range(ways):
+        part = lax.dynamic_slice_in_dim(x, (here ^ mask) * width, width, axis=split)
+        if mask:
+            part = lax.ppermute(part, axis, [(d, d ^ mask) for d in range(ways)])
+        full = lax.dynamic_update_slice_in_dim(full, part, (here ^ mask) * height, axis=join)
+    return full
 
 
 def layer_norm(values, norm_gain, norm_shift):
@@ -126,13 +142,7 @@
         .set(jnp.repeat(grad_slots, copies, axis=0))
     )
     arrived, grad_result = (
-        lax.all_to_all(
-            rows_send.reshape(row_count, slots, model_width),
-            "rows",
-            split_axis=0,
-            concat_axis=0,
-            tiled=True,
-        ),
+        exchange_in_pairs(rows_send.reshape(row_count, slots, model_width), "rows", 0, 0),
         lax.all_to_all(
             grads_send.reshape(row_count, slots, model_width),
             "rows",

time: 605 us -> 578 us (0.955)
  waiting for transfers between devices: 292 us -> 240 us
  local copies, waits for them, and re-layouts: 68.5 us -> 84.5 us
  starting transfers between devices: 36.9 us -> 46 us
    psum x1, waiting for transfers between devices: 46.3 us -> 9.37 us  [body(): lax.psum((router_grad, ln1_gain_grad, ln1_shift_grad, ln2_gain_grad, ln2_...]
    ppermute x0 -> x15, starting transfers between devices: none -> 27.7 us  [exchange_in_pairs(): part = lax.ppermute(part, axis, [(d, d ^ mask) for d in range(ways)])]
    all_to_all x1 -> x0, waiting for transfers between devices: 15.5 us -> none  [body(): lax.all_to_all(rows_send.reshape(row_count, slots, model_width), 'rows',...]
    dynamic_update_slice x0 -> x15, local copies, waits for them, and re-layouts: none -> 9.35 us  [exchange_in_pairs(): lax.dynamic_update_slice_in_dim(full, part, (here ^ mask) * height, axis=...]
    reduce_scatter x1, starting transfers between devices: 8.75 us -> 0.45 us  [body(): lax.psum_scatter(dot_last(grad_pre_low, expert_in).astype(jnp.bfloat16),...]
    all_to_all x1 -> x0, starting transfers between devices: 8.28 us -> none  [body(): lax.all_to_all(rows_send.reshape(row_count, slots, model_width), 'rows',...]
    unnamed x108 -> x98, local copies, waits for them, and re-layouts: 30.5 us -> 31.9 us
  transfers between devices with their start and end apart: 12 -> 26, of which waited for: 7 -> 7; matrix products, arithmetic and copies ran while one was open for 19% -> 27% of each run, Pallas kernels for 0% -> 0%
where the time goes in v1:
time: 578 us; the launch traced here: 571 us
  waiting for transfers between devices  240 us (42%)
  matrix products  104 us (18%)
  local copies, waits for them, and re-layouts  84.5 us (15%)
  blocking collectives  53.1 us (9%)
  starting transfers between devices  46 us (8%)
  other arithmetic  27.9 us (5%)
  between operations  16 us (3%)
    psum x1, waiting for transfers between devices, body(): qkv_grad, out_grad = lax.psum((qkv_grad, out_grad), 'rows')  187 us
    psum x1, blocking collectives, body(): lax.psum((router_grad, ln1_gain_grad, ln1_shift_grad, ln2_gain_grad, ln2_...  39.6 us
    dot_general x1, matrix products, body(): jnp.dot(both_rows, expert_in, preferred_element_type=jnp.float32) * mask  35.3 us
    unnamed x98, local copies, waits for them, and re-layouts  31.9 us
    ppermute x15, starting transfers between devices, exchange_in_pairs(): part = lax.ppermute(part, axis, [(d, d ^ mask) for d in range(ways)])  27.7 us
    dot_general x5, matrix products, dot_rows(): lax.dot_general(first_side, second_side, (((0,), (0,)), ((), ())), prefer...  26.8 us
    dot_general x5, matrix products, dot_last(): lax.dot_general(first_side, second_side, (((1,), (1,)), ((), ())), prefer...  22.9 us
    all_to_all x1, waiting for transfers between devices, body(): lax.all_to_all(grads_send.reshape(row_count, slots, model_width), 'rows',...  15.1 us
  transfers between devices with their start and end apart: 26, of which 7 were waited for; matrix products, arithmetic and copies ran while one was open for 27% of the time, Pallas kernels for 0%

profile of v1, /device:TPU:0, one launch (start us, length us, event | category | flops | bytes accessed | tf_op | source)
XLA Modules:
  0.0 571.0 jit_solution(5984266279915376749)
XLA Ops:
  17.8 7.0 %fusion.72 = (bf16[2,197,6,1,64]{4,3,2,1,0:T(2,128)(2,1)S(1)}, bf16[2,197,6,1,64]{4,3,2,1,0:T(2,128)(2,1)}, bf16[2,197,6,1,64]{4,3,2,1,0:T(2,128)(2,1)}) fusion(bf16[2,197,6,3,64]{4,3,2,1,0:T(4,128)(2,1)} %reshape.405), kind=kLoop, calls=%fused_computation.192 | loop fusion | bytes 1815552 | tf_op jit(solution)/shard_map/slice | solution.py:94
  27.3 3.7 copy.122
  41.9 5.2 fusion
  58.7 3.5 concatenate
  68.9 3.6 scatter_custom_fusion
  87.3 2.9 collective-permute-start.7
  92.8 3.5 collective-permute-start.9
  97.6 3.9 collective-permute-start.11
  103.8 4.6 collective-permute-start.13
  112.1 4.5 collective-permute-done.14
  117.6 3.2 scatter_custom_fusion.1
  120.8 3.6 all-to-all-start.1
  124.5 15.1 %all-to-all-done.1 = bf16[16,32,768]{2,1,0:T(8,128)(2,1)S(1)} async-done(((bf16[16,32,768]{2,1,0:T(8,128)(2,1)}), bf16[16,32,768]{2,1,0:T(8,128)(2,1)S(1)}, u32[]{:S(2)}, u32[]{:S(2)}) %all-to-all-start.1) | async-done | bytes 786464 | tf_op jit(solution)/shard_map/all_to_all | solution.py:146
  140.9 35.3 %fusion.5 = (bf16[1024,3072]{1,0:T(8,128)(2,1)S(1)}, f32[1024,3072]{1,0:T(8,128)}) fusion(s32[3072]{0:T(1024)S(1)} %add_select_fusion, s32[1024]{0:T(1024)S(1)} %add_select_fusion.1, bf16[1024,768]{1,0:T(8,128)(2,1)} %all-gather.5.cloned.1.call-done, bf16[768,3072]{1,0:T(8,128)(2,1)} %param.20), kind=kOutput, calls=%fused_computation.11 | convolution fusion | flops 5042601984 | bytes 25182208 | tf_op jit(solution)/shard_map/dot_general | solution.py:166
  178.9 8.5 %convolution_convert_fusion.2 = bf16[1024,768]{1,0:T(8,128)(2,1)} fusion(bf16[1024,3072]{1,0:T(8,128)(2,1)S(1)} %get-tuple-element.53, bf16[3072,768]{1,0:T(8,128)(2,1)} %param.21), kind=kOutput, calls=%fused_computation.39 | convolution fusion | flops 4832624640 | bytes 12582912 | tf_op jit(solution)/shard_map/dot_general | solution.py:169
  187.9 12.1 %fusion.2 = bf16[1024,3072]{1,0:T(8,128)(2,1)S(1)} fusion(f32[1024,3072]{1,0:T(8,128)} %get-tuple-element.54, bf16[1024,768]{1,0:T(8,128)(2,1)} %all-gather.7.cloned.1.call-done, bf16[3072,768]{1,0:T(8,128)(2,1)} %param.21, s32[3072]{0:T(1024)S(1)} %add_select_fusion, s32[1024]{0:T(1024)S(1)} %add_select_fusion.1), kind=kOutput, calls=%fused_computation.8 | convolution fusion | flops 4872732672 | bytes 25182208 | tf_op jit(solution)/shard_map/dot_general | solution.py:48
  202.7 6.3 %convolution_convert_fusion.1 = bf16[1024,768]{1,0:T(8,128)(2,1)} fusion(bf16[1024,3072]{1,0:T(8,128)(2,1)S(1)} %fusion.2, bf16[768,3072]{1,0:T(8,128)(2,1)S(1)} %bitcast.116), kind=kOutput, calls=%fused_computation.38 | convolution fusion | flops 4832624640 | bytes 12582912 | tf_op jit(solution)/shard_map/dot_general | solution.py:48
  209.0 4.6 all-to-all-start
  213.6 3.5 reduce-scatter.9.cloned.1.call-done
  217.1 14.4 %all-to-all-done = bf16[16,32,768]{2,1,0:T(8,128)(2,1)S(1)} async-done(((bf16[16,32,768]{2,1,0:T(8,128)(2,1)}), bf16[16,32,768]{2,1,0:T(8,128)(2,1)S(1)}, u32[]{:S(2)}, u32[]{:S(2)}) %all-to-all-start) | async-done | bytes 786464 | tf_op jit(solution)/shard_map/all_to_all | solution.py:184
  231.5 4.4 all-to-all-start.2
  243.3 4.7 multiply_reduce_fusion.2
  249.0 5.5 all-to-all-done.2
  259.9 3.5 reduce_sum.212
  283.9 4.6 fusion.75
  290.0 10.0 %fusion.79 = f32[3072,768]{1,0:T(8,128)} fusion(bf16[1024,3072]{1,0:T(8,128)(2,1)} %copy-done.39, bf16[1024,768]{1,0:T(8,128)(2,1)} %all-gather.7.cloned.1.call-done), kind=kOutput, calls=%fused_computation.199 | convolution fusion | flops 4831838208 | bytes 17301504 | tf_op jit(solution)/shard_map/dot_general | solution.py:42
  301.3 3.4 fusion.1
  308.1 9.9 %fusion.78 = f32[768,3072]{1,0:T(8,128)} fusion(bf16[1024,768]{1,0:T(8,128)(2,1)} %all-gather.5.cloned.1.call-done, bf16[1024,3072]{1,0:T(8,128)(2,1)} %copy-done.38), kind=kOutput, calls=%fused_computation.198 | convolution fusion | flops 4831838208 | bytes 17301504 | tf_op jit(solution)/shard_map/dot_general | solution.py:42
  320.8 39.6 %all-reduce.5 = (f32[768]{0:T(1024)}, f32[768]{0:T(1024)}, f32[768]{0:T(1024)}, f32[768]{0:T(1024)}) all-reduce(f32[768]{0:T(1024)S(1)} %get-tuple-element.15, f32[768]{0:T(1024)S(1)} %get-tuple-element.18, f32[768]{0:T(1024)S(1)} %get-tuple-element.11, ...), channel_id=1, replica_groups=mesh['rows'=16,'cols'=2] {'rows','cols'}, use_global_device_ids=true, to_apply=%region_29.30 | all-reduce | flops 3072 | bytes 24576 | tf_op jit(solution)/shard_map/psum | solution.py:260
  361.6 9.4 %all-reduce.10.cloned.1.call-done = f32[768,32]{0,1:T(8,128)} async-done(((f32[768,32]{0,1:T(8,128)}), f32[768,32]{0,1:T(8,128)}) %all-reduce.10.cloned.1.call-update) | async-done | bytes 98320 | tf_op jit(solution)/shard_map/psum | solution.py:260
  370.9 187.2 %all-reduce.12.cloned.1.call-done = (f32[768,1152]{1,0:T(8,128)}, f32[384,768]{1,0:T(8,128)}) async-done(((f32[768,1152]{1,0:T(8,128)}, f32[384,768]{1,0:T(8,128)}), (f32[768,1152]{1,0:T(8,128)}, f32[384,768]{1,0:T(8,128)})) %all-reduce.12.cloned.1.call-update) | async-done | bytes 4718608 | tf_op jit(solution)/shard_map/psum | solution.py:259
  558.1 4.1 copy.146
  (236 shorter events, 119.7 us)
Async XLA Ops:
  7.2 133.7 %all-gather.5.cloned.1.call-start = ((), (), s32[]{:S(2)}) async-start(), calls=%async_computation.5 | async-start | bytes 2359296 | tf_op jit(solution)/shard_map/all_gather | solution.py:158
  39.1 23.1 %copy-start.5 = (bf16[197,768]{1,0:T(8,128)(2,1)S(1)}, bf16[197,768]{1,0:T(8,128)(2,1)}, u32[]{:S(2)}) copy-start(bf16[197,768]{1,0:T(8,128)(2,1)} %param.12) | copy-start | bytes 907780
  41.9 22.4 %copy-start.30 = (f32[768]{0:T(1024)S(1)}, f32[768]{0:T(1024)}, u32[]{:S(2)}) copy-start(f32[768]{0:T(1024)} %param.17) | copy-start | bytes 9220
  47.1 11.6 %collective-permute-start.15 = (f32[3,768]{1,0:T(4,128)S(1)}, f32[3,768]{1,0:T(4,128)S(1)}, u32[]{:S(2)}, u32[]{:S(2)}) collective-permute-start(f32[3,768]{1,0:T(4,128)S(1)} %slice.33), channel_id=1, source_target_pairs={{0,1},{2,3},{4,5},{6,7},{8,9},{10,11},{12,13},{14,15},{16,17},{18,... | collective-permute-start | bytes 27656
  58.7 24.4 %copy-start.26 = (bf16[768,32]{0,1:T(8,128)(2,1)S(1)}, bf16[768,32]{0,1:T(8,128)(2,1)}, u32[]{:S(2)}) copy-start(bf16[768,32]{0,1:T(8,128)(2,1)} %param.19) | copy-start | bytes 147460
  65.1 55.7 %copy-start.11 = (bf16[197,768]{1,0:T(8,128)(2,1)}, bf16[197,768]{1,0:T(8,128)(2,1)S(1)}, u32[]{:S(2)}) copy-start(bf16[197,768]{1,0:T(8,128)(2,1)S(1)} %add_convert_fusion.2) | copy-start | bytes 907780
  75.3 8.1 %collective-permute-start = (bf16[1,32,768]{2,1,0:T(8,128)(2,1)S(1)}, bf16[1,32,768]{2,1,0:T(8,128)(2,1)S(1)}, u32[]{:S(2)}, u32[]{:S(2)}) collective-permute-start(bf16[1,32,768]{2,1,0:T(8,128)(2,1)S(1)} %get-tuple-element.46), channel_id=1, source_target_pairs={{0,2},{2,0},{4,6},{6,4},{8,10},{10,8},{12,14},{14,12},{16,18},{18,... | collective-permute-start | bytes 147464 | tf_op jit(solution)/shard_map/ppermute | solution.py:23
  78.2 8.5 %collective-permute-start.1 = (bf16[1,32,768]{2,1,0:T(8,128)(2,1)S(1)}, bf16[1,32,768]{2,1,0:T(8,128)(2,1)S(1)}, u32[]{:S(2)}, u32[]{:S(2)}) collective-permute-start(bf16[1,32,768]{2,1,0:T(8,128)(2,1)S(1)} %get-tuple-element.45), channel_id=1, source_target_pairs={{0,4},{2,6},{4,0},{6,2},{8,12},{10,14},{12,8},{14,10},{16,20},{18,... | collective-permute-start | bytes 147464 | tf_op jit(solution)/shard_map/ppermute | solution.py:23
  79.7 7.6 %collective-permute-start.2 = (bf16[1,32,768]{2,1,0:T(8,128)(2,1)S(1)}, bf16[1,32,768]{2,1,0:T(8,128)(2,1)S(1)}, u32[]{:S(2)}, u32[]{:S(2)}) collective-permute-start(bf16[1,32,768]{2,1,0:T(8,128)(2,1)S(1)} %get-tuple-element.44), channel_id=1, source_target_pairs={{0,6},{2,4},{4,2},{6,0},{8,14},{10,12},{12,10},{14,8},{16,22},{18,... | collective-permute-start | bytes 147464 | tf_op jit(solution)/shard_map/ppermute | solution.py:23
  79.7 11.2 %collective-permute-start.3 = (bf16[1,32,768]{2,1,0:T(8,128)(2,1)S(1)}, bf16[1,32,768]{2,1,0:T(8,128)(2,1)S(1)}, u32[]{:S(2)}, u32[]{:S(2)}) collective-permute-start(bf16[1,32,768]{2,1,0:T(8,128)(2,1)S(1)} %get-tuple-element.43), channel_id=1, source_target_pairs={{0,8},{2,10},{4,12},{6,14},{8,0},{10,2},{12,4},{14,6},{16,24},{18,... | collective-permute-start | bytes 147464 | tf_op jit(solution)/shard_map/ppermute | solution.py:23
  81.7 11.0 %collective-permute-start.4 = (bf16[1,32,768]{2,1,0:T(8,128)(2,1)S(1)}, bf16[1,32,768]{2,1,0:T(8,128)(2,1)S(1)}, u32[]{:S(2)}, u32[]{:S(2)}) collective-permute-start(bf16[1,32,768]{2,1,0:T(8,128)(2,1)S(1)} %get-tuple-element.42), channel_id=1, source_target_pairs={{0,10},{2,8},{4,14},{6,12},{8,2},{10,0},{12,6},{14,4},{16,26},{18,... | collective-permute-start | bytes 147464 | tf_op jit(solution)/shard_map/ppermute | solution.py:23
  83.4 13.5 %collective-permute-start.5 = (bf16[1,32,768]{2,1,0:T(8,128)(2,1)S(1)}, bf16[1,32,768]{2,1,0:T(8,128)(2,1)S(1)}, u32[]{:S(2)}, u32[]{:S(2)}) collective-permute-start(bf16[1,32,768]{2,1,0:T(8,128)(2,1)S(1)} %get-tuple-element.41), channel_id=1, source_target_pairs={{0,12},{2,14},{4,8},{6,10},{8,4},{10,6},{12,0},{14,2},{16,28},{18,... | collective-permute-start | bytes 147464 | tf_op jit(solution)/shard_map/ppermute | solution.py:23
  86.7 10.9 %collective-permute-start.6 = (bf16[1,32,768]{2,1,0:T(8,128)(2,1)S(1)}, bf16[1,32,768]{2,1,0:T(8,128)(2,1)S(1)}, u32[]{:S(2)}, u32[]{:S(2)}) collective-permute-start(bf16[1,32,768]{2,1,0:T(8,128)(2,1)S(1)} %get-tuple-element.40), channel_id=1, source_target_pairs={{0,14},{2,12},{4,10},{6,8},{8,6},{10,4},{12,2},{14,0},{16,30},{18,... | collective-permute-start | bytes 147464 | tf_op jit(solution)/shard_map/ppermute | solution.py:23
  87.3 14.7 %collective-permute-start.7 = (bf16[1,32,768]{2,1,0:T(8,128)(2,1)S(1)}, bf16[1,32,768]{2,1,0:T(8,128)(2,1)S(1)}, u32[]{:S(2)}, u32[]{:S(2)}) collective-permute-start(bf16[1,32,768]{2,1,0:T(8,128)(2,1)S(1)} %get-tuple-element.39), channel_id=1, source_target_pairs={{0,16},{2,18},{4,20},{6,22},{8,24},{10,26},{12,28},{14,30},{16,0},... | collective-permute-start | bytes 147464 | tf_op jit(solution)/shard_map/ppermute | solution.py:23
  90.9 12.9 %collective-permute-start.8 = (bf16[1,32,768]{2,1,0:T(8,128)(2,1)S(1)}, bf16[1,32,768]{2,1,0:T(8,128)(2,1)S(1)}, u32[]{:S(2)}, u32[]{:S(2)}) collective-permute-start(bf16[1,32,768]{2,1,0:T(8,128)(2,1)S(1)} %get-tuple-element.38), channel_id=1, source_target_pairs={{0,18},{2,16},{4,22},{6,20},{8,26},{10,24},{12,30},{14,28},{16,2},... | collective-permute-start | bytes 147464 | tf_op jit(solution)/shard_map/ppermute | solution.py:23
  92.8 16.2 %collective-permute-start.9 = (bf16[1,32,768]{2,1,0:T(8,128)(2,1)S(1)}, bf16[1,32,768]{2,1,0:T(8,128)(2,1)S(1)}, u32[]{:S(2)}, u32[]{:S(2)}) collective-permute-start(bf16[1,32,768]{2,1,0:T(8,128)(2,1)S(1)} %get-tuple-element.37), channel_id=1, source_target_pairs={{0,20},{2,22},{4,16},{6,18},{8,28},{10,30},{12,24},{14,26},{16,4},... | collective-permute-start | bytes 147464 | tf_op jit(solution)/shard_map/ppermute | solution.py:23
  96.9 12.7 %collective-permute-start.10 = (bf16[1,32,768]{2,1,0:T(8,128)(2,1)S(1)}, bf16[1,32,768]{2,1,0:T(8,128)(2,1)S(1)}, u32[]{:S(2)}, u32[]{:S(2)}) collective-permute-start(bf16[1,32,768]{2,1,0:T(8,128)(2,1)S(1)} %get-tuple-element.36), channel_id=1, source_target_pairs={{0,22},{2,20},{4,18},{6,16},{8,30},{10,28},{12,26},{14,24},{16,6},... | collective-permute-start | bytes 147464 | tf_op jit(solution)/shard_map/ppermute | solution.py:23
  97.6 12.7 %collective-permute-start.11 = (bf16[1,32,768]{2,1,0:T(8,128)(2,1)S(1)}, bf16[1,32,768]{2,1,0:T(8,128)(2,1)S(1)}, u32[]{:S(2)}, u32[]{:S(2)}) collective-permute-start(bf16[1,32,768]{2,1,0:T(8,128)(2,1)S(1)} %get-tuple-element.35), channel_id=1, source_target_pairs={{0,24},{2,26},{4,28},{6,30},{8,16},{10,18},{12,20},{14,22},{16,8},... | collective-permute-start | bytes 147464 | tf_op jit(solution)/shard_map/ppermute | solution.py:23
  102.0 8.9 %collective-permute-start.12 = (bf16[1,32,768]{2,1,0:T(8,128)(2,1)S(1)}, bf16[1,32,768]{2,1,0:T(8,128)(2,1)S(1)}, u32[]{:S(2)}, u32[]{:S(2)}) collective-permute-start(bf16[1,32,768]{2,1,0:T(8,128)(2,1)S(1)} %get-tuple-element.34), channel_id=1, source_target_pairs={{0,26},{2,24},{4,30},{6,28},{8,18},{10,16},{12,22},{14,20},{16,10}... | collective-permute-start | bytes 147464 | tf_op jit(solution)/shard_map/ppermute | solution.py:23
  103.8 7.7 %collective-permute-start.13 = (bf16[1,32,768]{2,1,0:T(8,128)(2,1)S(1)}, bf16[1,32,768]{2,1,0:T(8,128)(2,1)S(1)}, u32[]{:S(2)}, u32[]{:S(2)}) collective-permute-start(bf16[1,32,768]{2,1,0:T(8,128)(2,1)S(1)} %get-tuple-element.33), channel_id=1, source_target_pairs={{0,28},{2,30},{4,24},{6,26},{8,20},{10,22},{12,16},{14,18},{16,12}... | collective-permute-start | bytes 147464 | tf_op jit(solution)/shard_map/ppermute | solution.py:23
  109.0 7.7 %collective-permute-start.14 = (bf16[1,32,768]{2,1,0:T(8,128)(2,1)S(1)}, bf16[1,32,768]{2,1,0:T(8,128)(2,1)S(1)}, u32[]{:S(2)}, u32[]{:S(2)}) collective-permute-start(bf16[1,32,768]{2,1,0:T(8,128)(2,1)S(1)} %get-tuple-element.32), channel_id=1, source_target_pairs={{0,30},{2,28},{4,26},{6,24},{8,22},{10,20},{12,18},{14,16},{16,14}... | collective-permute-start | bytes 147464 | tf_op jit(solution)/shard_map/ppermute | solution.py:23
  120.8 18.9 %all-to-all-start.1 = ((bf16[16,32,768]{2,1,0:T(8,128)(2,1)}), bf16[16,32,768]{2,1,0:T(8,128)(2,1)S(1)}, u32[]{:S(2)}, u32[]{:S(2)}) async-start(bf16[16,32,768]{2,1,0:T(8,128)(2,1)} %bitcast.108), calls=%async_computation.2 | async-start | bytes 1572864 | tf_op jit(solution)/shard_map/all_to_all | solution.py:146
  124.4 63.4 %all-gather.7.cloned.1.call-start = ((), (), s32[]{:S(2)}) async-start(), calls=%async_computation.7 | async-start | bytes 2359296 | tf_op jit(solution)/shard_map/all_gather | solution.py:159
  140.6 68.4 %reduce-scatter.7.cloned.1.call-start = ((), (), s32[]{:S(2)}) async-start(), calls=%async_computation.6 | async-start | bytes 2359296 | tf_op jit(solution)/shard_map/reduce_scatter | solution.py:168
  178.9 23.8 %slice-start = ((s8[4718592]{0:T(1024)(128)(4,1)}), s8[524288]{0:T(1024)(128)(4,1)S(1)}, s32[]{:S(2)}) async-start(s8[4718592]{0:T(1024)(128)(4,1)} %bitcast.115), calls=%async_computation.11 | async-start | bytes 1048576
  187.4 29.7 %reduce-scatter.9.cloned.1.call-start = ((), (), s32[]{:S(2)}) async-start(), calls=%async_computation.8 | async-start | bytes 2359296 | tf_op jit(solution)/shard_map/reduce_scatter | solution.py:178
  209.0 22.5 %all-to-all-start = ((bf16[16,32,768]{2,1,0:T(8,128)(2,1)}), bf16[16,32,768]{2,1,0:T(8,128)(2,1)S(1)}, u32[]{:S(2)}, u32[]{:S(2)}) async-start(bf16[16,32,768]{2,1,0:T(8,128)(2,1)} %bitcast.110), calls=%async_computation.1 | async-start | bytes 1572864 | tf_op jit(solution)/shard_map/all_to_all | solution.py:184
  231.5 22.9 %all-to-all-start.2 = ((bf16[16,32,768]{2,1,0:T(8,128)(2,1)}), bf16[16,32,768]{2,1,0:T(8,128)(2,1)S(1)}, u32[]{:S(2)}, u32[]{:S(2)}) async-start(bf16[16,32,768]{2,1,0:T(8,128)(2,1)} %bitcast.109), calls=%async_computation.4 | async-start | bytes 1572864 | tf_op jit(solution)/shard_map/all_to_all | solution.py:197
  235.9 135.1 %all-reduce.10.cloned.1.call-start = ((), (), s32[]{:S(2)}) async-start(), calls=%async_computation.9 | async-start | bytes 196608 | tf_op jit(solution)/shard_map/psum | solution.py:260
  248.9 309.2 %all-reduce.12.cloned.1.call-start = ((), (), s32[]{:S(2)}) async-start(), calls=%async_computation.10 | async-start | bytes 9437184 | tf_op jit(solution)/shard_map/psum | solution.py:259
  305.5 55.0 %copy-start.8 = (f32[197,768]{1,0:T(8,128)S(1)}, f32[197,768]{1,0:T(8,128)}, u32[]{:S(2)}) copy-start(f32[197,768]{1,0:T(8,128)} %copy-done.7) | copy-start | bytes 1815556
  305.5 12.5 %collective-permute-start.16 = (bf16[3,768]{1,0:T(4,128)(2,1)S(1)}, bf16[3,768]{1,0:T(4,128)(2,1)S(1)}, u32[]{:S(2)}, u32[]{:S(2)}) collective-permute-start(bf16[3,768]{1,0:T(4,128)(2,1)S(1)} %slice.34), channel_id=1, source_target_pairs={{0,1},{2,3},{4,5},{6,7},{8,9},{10,11},{12,13},{14,15},{16,17},{18,... | collective-permute-start | bytes 13832
  (36 other events, 269.5 us)
Sparse Core Ops, SparseCore 0:
  117.5 6.6 all-gather.4
  140.7 8.4 all-gather.6
  187.5 7.7 reduce-scatter.6
  209.1 8.0 reduce-scatter.8
  249.0 121.8 all-reduce.9
  377.1 180.9 all-reduce.11
